TPU v7x, 32 devices: a whole 2x2x4 slice. The times are simulated.
32 devices in a mesh: groups: 2 (over y), mom: 4 (over z), lat: 2 (over x), band: 2 (over core).
Axes of the slice: x: 2, y: 2, z: 4, core: 2. Of those that a mesh axis runs over, the one named last changes fastest.
Arguments:
- table: bfloat16 [2048, 2, 32, 32], P(('groups', 'mom', 'lat'), None, None, 'band'), parts along dimension 0, may hold values from -0.1875 to 0.1875
- lattice: int32 [1024, 6], P(('mom', 'lat')), may hold values from -6 to 6
- pairs: int32 [6, 4096], P(None, ('groups', 'mom')), parts along dimension 1, may hold values from 0 to 23
- left_rot: float32 [4096, 2, 32, 32], P(('groups', 'mom', 'lat')), parts along dimension 0, may hold values from -0.75 to 0.75
- right_rotation: float32 [4096, 2, 32, 32], P(('groups', 'mom', 'lat'), None, 'band'), parts along dimension 0, may hold values from -0.75 to 0.75
Outputs:
- coupling: float32 [4096, 2, 32, 32], P(('groups', 'mom', 'lat'), None, None, 'band'), parts along dimension 0
There are 2 independent parts, one for each index of `groups`. A program takes and returns all parts, laid end to end along the dimension named above; an argument that names none is the same for every part. Nothing has to cross between parts.
All inputs are finite; a program needn't handle non-finite values.
Results may differ from a plain program's by a relative error of at most 0.0018.
Values may be sent and summed in bfloat16 or wider, within the bound.
A program may use at most 128 MiB of HBM per device.

v0:
```python
import functools
import math

import jax
import jax.numpy as jnp
import numpy as np
from jax import lax
from jax.experimental import pallas as pl
from jax.experimental.pallas import tpu as pltpu
from jax.sharding import PartitionSpec as P

NK = 24
F32 = jnp.float32
BF16 = jnp.bfloat16


def _sine_fit():
    b = 6.0 * np.sin(np.linspace(1e-3, math.pi / 2, 400))
    cols = np.stack([b ** (2 * j + 1) for j in range(5)], 1)
    scale = np.abs(cols).max(0)
    sol = np.linalg.lstsq(cols / scale, np.sin(math.pi * b / 12), rcond=None)[0]
    return [float(np.float32(v)) for v in sol / scale]


SINE = _sine_fit()


def quarter_sine(b):
    x = b * b
    acc = x * SINE[4] + SINE[3]
    acc = acc * x + SINE[2]
    acc = acc * x + SINE[1]
    acc = acc * x + SINE[0]
    return acc * b


def loop(count, body):
    if count <= 4:
        for i in range(count):
            body(i)
    else:
        def step(i, carry):
            body(i)
            return carry
        lax.fori_loop(0, count, step, 0)


def kernel(
    cfg, table, lattice, pairs, left, right, out,
    gath, lats, phase_a, phase_b, bloch, lbuf, rbuf, rother, tmine, tother,
    lat_send, lat_recv, tab_send, tab_recv, own_sem, in_sem, swap_send, swap_recv,
):
    moms, lat_n, chunks, mc, nb_loc, owned, bands = cfg
    shards = moms * lat_n
    z = lax.axis_index("mom")
    x = lax.axis_index("lat")
    core = lax.axis_index("band")
    me = z * lat_n + x
    other = 1 - core
    rloc = table.shape[3]
    lane_tiles = owned // 128

    lcopy = pltpu.make_async_copy(left, lbuf, in_sem.at[0])
    rcopy = pltpu.make_async_copy(right, rbuf, in_sem.at[1])
    lcopy.start()
    rcopy.start()

    barrier = pltpu.get_barrier_semaphore()

    def greet(q, carry):
        @pl.when(q != me)
        def _():
            pl.semaphore_signal(
                barrier, inc=1,
                device_id={"mom": q // lat_n, "lat": q % lat_n},
                device_id_type=pl.DeviceIdType.MESH,
            )
        return carry

    lax.fori_loop(0, shards, greet, 0)
    pl.semaphore_signal(
        barrier, inc=1, device_id={"band": other},
        device_id_type=pl.DeviceIdType.MESH,
    )
    pl.semaphore_wait(barrier, shards)

    def lat_copy(q, slot, sem_at):
        return pltpu.make_async_remote_copy(
            src_ref=lattice, dst_ref=lats.at[slot],
            send_sem=lat_send.at[sem_at], recv_sem=lat_recv.at[slot],
            device_id={"mom": q // lat_n, "lat": q % lat_n},
            device_id_type=pl.DeviceIdType.MESH,
        )

    def lat_out(q, carry):
        @pl.when(q != me)
        def _():
            lat_copy(q, me, q).start()
        return carry

    lax.fori_loop(0, shards, lat_out, 0)
    lat_own = pltpu.make_async_copy(lattice, lats.at[me], own_sem.at[chunks])
    lat_own.start()

    def tab_copy(src, slot, c, way):
        step = 1 if way % 2 == 0 else -1
        dev = {"mom": z + step} if way < 2 else {"lat": x + step}
        return pltpu.make_async_remote_copy(
            src_ref=src, dst_ref=gath.at[c, slot],
            send_sem=tab_send.at[way, slot, c], recv_sem=tab_recv.at[slot, c],
            device_id=dev, device_id_type=pl.DeviceIdType.MESH,
        )

    def sent_ways(slot):
        j = slot // lat_n
        i = slot % lat_n
        return (
            (i == x) & (j <= z) & (z < moms - 1),
            (i == x) & (j >= z) & (z > 0),
            (i <= x) & (x < lat_n - 1),
            (i >= x) & (x > 0),
        )

    def pass_on(src, slot, c, ways=(0, 1, 2, 3)):
        conds = sent_ways(slot)
        for way in ways:
            @pl.when(conds[way])
            def _(way=way):
                tab_copy(src, slot, c, way).start()

    for c in range(chunks):
        pass_on(table.at[:, pl.ds(c * mc, mc)], me, c)
    own = [
        pltpu.make_async_copy(
            table.at[:, pl.ds(c * mc, mc)], gath.at[c, me], own_sem.at[c]
        )
        for c in range(chunks)
    ]
    for c in range(chunks):
        own[c].start()

    half = nb_loc
    rcopy.wait()
    rswap = pltpu.make_async_remote_copy(
        src_ref=rbuf.at[:, :, pl.ds(pl.multiple_of(other * half, 8), half)],
        dst_ref=rother, send_sem=swap_send.at[0], recv_sem=swap_recv.at[0],
        device_id={"band": other}, device_id_type=pl.DeviceIdType.MESH,
    )
    rswap.start()

    lat_own.wait()
    kq = pairs[:, pl.ds(pl.multiple_of(x * owned, 128), owned)]
    kq = kq.astype(F32).astype(BF16)

    def phase(q, carry):
        @pl.when(q != me)
        def _():
            lat_copy(q, q, q).wait_recv()

        comp = lats[q].astype(F32).astype(BF16)
        turn = lax.dot_general(
            comp, kq, (((0,), (0,)), ((), ())), preferred_element_type=F32
        )
        turn = turn - jnp.round(turn * (1.0 / NK)) * NK
        cosine = quarter_sine(6.0 - jnp.abs(turn))
        folded = jnp.maximum(jnp.minimum(turn, 12.0 - turn), -12.0 - turn)
        sine = quarter_sine(folded)
        cb = cosine.astype(BF16)
        rows = pl.ds(pl.multiple_of(q * rloc, rloc), rloc)
        phase_a[rows, :owned] = cb
        phase_a[rows, owned:] = sine.astype(BF16)
        phase_b[rows, :owned] = (-sine).astype(BF16)
        phase_b[rows, owned:] = cb
        return carry

    lax.fori_loop(0, shards, phase, 0)

    def along_mom(step):
        dist = step + 1
        for c in range(chunks):
            for sign in (-1, 1):
                j = z + sign * dist

                @pl.when((j >= 0) & (j < moms))
                def _(j=j, c=c):
                    slot = j * lat_n + x
                    tab_copy(gath.at[c, slot], slot, c, 0).wait_recv()
                    pass_on(gath.at[c, slot], slot, c)

    loop(moms - 1, along_mom)

    def from_lat(c):
        for dist in range(1, lat_n):
            for sign in (-1, 1):
                i = x + sign * dist

                @pl.when((i >= 0) & (i < lat_n))
                def _(i=i):
                    def one(j):
                        slot = j * lat_n + i
                        tab_copy(gath.at[c, slot], slot, c, 2).wait_recv()
                        if lat_n > 2:
                            pass_on(gath.at[c, slot], slot, c, (2, 3))

                    loop(moms, one)

    lcopy.wait()
    group = math.gcd(shards, 8)
    kdim = group * rloc
    nblk = 4

    for c in range(chunks):
        own[c].wait()
        from_lat(c)

        def contract(g):
            pieces = [
                [gath[c, g * group + s, part].reshape(mc * nb_loc, rloc)
                 for s in range(group)]
                for part in (0, 1)
            ]
            rows = pl.ds(g * kdim, kdim)
            return jnp.dot(
                jnp.concatenate(pieces[0], 1), phase_a[rows, :],
                preferred_element_type=F32,
            ) + jnp.dot(
                jnp.concatenate(pieces[1], 1), phase_b[rows, :],
                preferred_element_type=F32,
            )

        bloch[...] = contract(0).reshape(bloch.shape)
        if shards > group:
            def add(g, carry):
                bloch[...] += contract(g).reshape(bloch.shape)
                return carry
            lax.fori_loop(1, shards // group, add, 0)

        def left_step(it, carry):
            eight = it // lane_tiles
            l0 = pl.multiple_of((it % lane_tiles) * 128, 128)
            lanes = pl.ds(l0, 128)
            lanes_im = pl.ds(l0 + owned, 128)
            for n0 in range(0, 8, nblk):
                tre = [None] * nblk
                tim = [None] * nblk
                for m in range(mc):
                    lre = lbuf[0, c * mc + m, :, lanes]
                    lim = lbuf[1, c * mc + m, :, lanes]
                    at = m * (nb_loc // 8) + eight
                    for n in range(nblk):
                        row = pl.ds(n0 + n, 1)
                        bre = jnp.broadcast_to(bloch[at, row, lanes], (bands, 128))
                        bim = jnp.broadcast_to(bloch[at, row, lanes_im], (bands, 128))
                        a = lre * bre + lim * bim
                        b = lre * bim - lim * bre
                        tre[n] = a if m == 0 else tre[n] + a
                        tim[n] = b if m == 0 else tim[n] + b
                for n in range(nblk):
                    col = eight * 8 + n0 + n
                    tr = tre[n].reshape(bands // 8, 8, 128)
                    ti = tim[n].reshape(bands // 8, 8, 128)
                    if c > 0:
                        tr = tr + tmine[0, col, :, :, lanes]
                        ti = ti + tmine[1, col, :, :, lanes]
                    tmine[0, col, :, :, lanes] = tr
                    tmine[1, col, :, :, lanes] = ti
            return carry

        lax.fori_loop(0, (nb_loc // 8) * lane_tiles, left_step, 0)

    tswap = pltpu.make_async_remote_copy(
        src_ref=tmine, dst_ref=tother,
        send_sem=swap_send.at[1], recv_sem=swap_recv.at[1],
        device_id={"band": other}, device_id_type=pl.DeviceIdType.MESH,
    )
    tswap.start()

    kblk = 8

    def right_half(tref, rref, row0, first):
        def body(it, carry):
            eight = it // lane_tiles
            k0 = eight * 8
            lanes = pl.ds(pl.multiple_of((it % lane_tiles) * 128, 128), 128)
            cre = [None] * kblk
            cim = [None] * kblk
            for n in range(nb_loc):
                vre = rref[0, n, pl.ds(row0, half), lanes]
                vim = rref[1, n, pl.ds(row0, half), lanes]
                for k in range(kblk):
                    row = pl.ds(k, 1)
                    tr = jnp.broadcast_to(tref[0, n, eight, row, lanes], (half, 128))
                    ti = jnp.broadcast_to(tref[1, n, eight, row, lanes], (half, 128))
                    a = tr * vre - ti * vim
                    b = tr * vim + ti * vre
                    cre[k] = a if n == 0 else cre[k] + a
                    cim[k] = b if n == 0 else cim[k] + b
            for k in range(kblk):
                if not first:
                    cre[k] = cre[k] + out[0, k0 + k, :, lanes]
                    cim[k] = cim[k] + out[1, k0 + k, :, lanes]
                out[0, k0 + k, :, lanes] = cre[k]
                out[1, k0 + k, :, lanes] = cim[k]
            return carry

        lax.fori_loop(0, (bands // kblk) * lane_tiles, body, 0)

    right_half(tmine, rbuf, pl.multiple_of(core * half, 8), True)
    rswap.wait_recv()
    tswap.wait_recv()
    right_half(tother, rother, 0, False)

    rswap.wait_send()
    tswap.wait_send()

    def lat_done(q, carry):
        @pl.when(q != me)
        def _():
            lat_copy(q, me, q).wait_send()
        return carry

    lax.fori_loop(0, shards, lat_done, 0)

    def tab_done(slot, carry):
        conds = sent_ways(slot)
        for c in range(chunks):
            for way in range(4):
                @pl.when(conds[way])
                def _(way=way, c=c):
                    tab_copy(gath.at[c, slot], slot, c, way).wait_send()
        return carry

    lax.fori_loop(0, shards, tab_done, 0)


def per_device(moms, lat_n, table, lattice, pairs, left_rot, right_rotation):
    tab = jnp.transpose(table, (1, 2, 3, 0))
    lat = jnp.transpose(lattice, (1, 0))
    lef = jnp.transpose(left_rot, (1, 2, 3, 0))
    rig = jnp.transpose(right_rotation, (1, 2, 3, 0))
    bands = tab.shape[1]
    nb_loc = tab.shape[2]
    rloc = tab.shape[3]
    owned = lef.shape[3]
    shards = moms * lat_n
    chunks = 4
    mc = bands // chunks
    cfg = (moms, lat_n, chunks, mc, nb_loc, owned, bands)
    anyspace = pl.BlockSpec(memory_space=pl.ANY)
    vmem = pl.BlockSpec(memory_space=pltpu.VMEM)
    dma = pltpu.SemaphoreType.DMA
    res = pl.pallas_call(
        functools.partial(kernel, cfg),
        out_shape=jax.ShapeDtypeStruct((2, bands, nb_loc, owned), F32),
        in_specs=[anyspace, anyspace, vmem, anyspace, anyspace],
        out_specs=vmem,
        scratch_shapes=[
            pltpu.VMEM((chunks, shards, 2, mc, nb_loc, rloc), BF16),
            pltpu.VMEM((shards, lat.shape[0], rloc), jnp.int32),
            pltpu.VMEM((shards * rloc, 2 * owned), BF16),
            pltpu.VMEM((shards * rloc, 2 * owned), BF16),
            pltpu.VMEM((mc * nb_loc // 8, 8, 2 * owned), F32),
            pltpu.VMEM(lef.shape, F32),
            pltpu.VMEM(rig.shape, F32),
            pltpu.VMEM((2, nb_loc, nb_loc, owned), F32),
            pltpu.VMEM((2, nb_loc, bands // 8, 8, owned), F32),
            pltpu.VMEM((2, nb_loc, bands // 8, 8, owned), F32),
            dma((shards,)),
            dma((shards,)),
            dma((4, shards, chunks)),
            dma((shards, chunks)),
            dma((chunks + 1,)),
            dma((2,)),
            dma((2,)),
            dma((2,)),
        ],
        compiler_params=pltpu.CompilerParams(
            collective_id=0, has_side_effects=True,
            vmem_limit_bytes=60 * 1024 * 1024,
        ),
    )(tab, lat, pairs, lef, rig)
    return jnp.transpose(res, (3, 0, 1, 2))


def solution(mesh):
    in_specs = (
        P(("groups", "mom", "lat"), None, None, "band"),
        P(("mom", "lat"), None),
        P(None, ("groups", "mom")),
        P(("groups", "mom", "lat"), None, None, None),
        P(("groups", "mom", "lat"), None, "band", None),
    )
    out_specs = P(("groups", "mom", "lat"), None, None, "band")
    body = functools.partial(per_device, mesh.shape["mom"], mesh.shape["lat"])
    return jax.shard_map(
        body, mesh=mesh, in_specs=in_specs, out_specs=out_specs, check_vma=False
    )
```

profile of v0, /device:TPU:0, one launch (start us, length us, event | category | flops | bytes accessed | tf_op | source)
XLA Modules:
  0.0 46.7 jit_solution(3933965037441215383)
XLA Ops:
  0.0 44.4 %shard_map.55 = f32[2,32,16,256]{3,2,1,0:T(8,128)} custom-call(bf16[2,32,16,128]{3,2,1,0:T(8,128)(2,1)} %bitcast.8, s32[6,128]{1,0:T(8,128)} %bitcast.9, s32[6,512]{1,0:T(8,128)} %pairs.1, f32[2,32,32,256]{3,2,1,0:T(8,128)} %bitcast.6, f32[2,16,32,256]{3,2,1,0:T(8,128)} %bitcast.7), custom_call_target="tpu_custom_call" | custom-call | tf_op jit(solution)/shard_map/pallas_call | solution.py:352
  44.4 2.3 %copy.7 = f32[256,2,32,16]{0,3,2,1:T(8,128)} copy(f32[256,2,32,16]{0,3,2,1:T(8,128)} %bitcast.5) | data formatting | bytes 2097152
where the time goes:
time: 46.9 us; the launch traced here: 46.7 us
  Pallas kernels  44.4 us (95%)
  local copies, waits for them, and re-layouts  2.26 us (5%)
    pallas_call x1, Pallas kernels, per_device(): pl.pallas_call(functools.partial(kernel, cfg), out_shape=jax.ShapeDtypeSt...  44.4 us
    unnamed x1, local copies, waits for them, and re-layouts  2.26 us

commit v1 on v0

v1 whole, which is shorter than its diff:
```python
import functools
import math

import jax
import jax.numpy as jnp
import numpy as np
from jax import lax
from jax.experimental import pallas as pl
from jax.experimental.pallas import tpu as pltpu
from jax.sharding import PartitionSpec as P

NK = 24
LAG = 1
F32 = jnp.float32
BF16 = jnp.bfloat16


def _sine_fit():
    b = 6.0 * np.sin(np.linspace(1e-3, math.pi / 2, 400))
    cols = np.stack([b ** (2 * j + 1) for j in range(5)], 1)
    scale = np.abs(cols).max(0)
    sol = np.linalg.lstsq(cols / scale, np.sin(math.pi * b / 12), rcond=None)[0]
    return [float(np.float32(v)) for v in sol / scale]


SINE = _sine_fit()


def quarter_sine(b):
    x = b * b
    acc = x * SINE[4] + SINE[3]
    acc = acc * x + SINE[2]
    acc = acc * x + SINE[1]
    acc = acc * x + SINE[0]
    return acc * b


def loop(count, body):
    if count <= 4:
        for i in range(count):
            body(i)
    else:
        def step(i, carry):
            body(i)
            return carry
        lax.fori_loop(0, count, step, 0)


def kernel(
    cfg, table, lattice, pairs, left, right, out,
    gath, lats, phase_a, phase_b, bloch, bother, mids, lbuf, rbuf, rother,
    send_sem, mom_recv, lat_recv, own_sem, in_sem, swap_send, swap_recv,
):
    moms, lat_n, chunks, mc, nb_loc, owned, bands = cfg
    shards = moms * lat_n
    z = lax.axis_index("mom")
    x = lax.axis_index("lat")
    core = lax.axis_index("band")
    me = z * lat_n + x
    other = 1 - core
    rloc = table.shape[3]
    lane_tiles = owned // 128

    lcopy = pltpu.make_async_copy(left, lbuf, in_sem.at[0])
    rcopy = pltpu.make_async_copy(right, rbuf, in_sem.at[1])
    lcopy.start()
    rcopy.start()

    barrier = pltpu.get_barrier_semaphore()

    near = (
        (z < moms - 1, {"mom": z + 1}),
        (z > 0, {"mom": z - 1}),
        (x < lat_n - 1, {"lat": x + 1}),
        (x > 0, {"lat": x - 1}),
    )
    for cond, dev in near:
        @pl.when(cond)
        def _(dev=dev):
            pl.semaphore_signal(
                barrier, inc=1, device_id=dev,
                device_id_type=pl.DeviceIdType.MESH,
            )
    pl.semaphore_signal(
        barrier, inc=1, device_id={"band": other},
        device_id_type=pl.DeviceIdType.MESH,
    )
    pl.semaphore_wait(barrier, 1 + sum(c.astype(jnp.int32) for c, _ in near))

    lat_item = chunks

    def place(slot, c):
        return lats.at[slot] if c == lat_item else gath.at[c, slot]

    def tab_copy(src, slot, c, way):
        if way < 2:
            recv = mom_recv.at[slot // lat_n, c]
        else:
            recv = lat_recv.at[slot if lat_n > 2 else 0, c]
        return pltpu.make_async_remote_copy(
            src_ref=src, dst_ref=place(slot, c),
            send_sem=send_sem.at[way, int(c == lat_item)], recv_sem=recv,
            device_id=near[way][1], device_id_type=pl.DeviceIdType.MESH,
        )

    def sent_ways(slot):
        j = slot // lat_n
        i = slot % lat_n
        return (
            (i == x) & (j <= z) & (z < moms - 1),
            (i == x) & (j >= z) & (z > 0),
            (i <= x) & (x < lat_n - 1),
            (i >= x) & (x > 0),
        )

    def pass_on(src, slot, c, ways=(0, 1, 2, 3)):
        conds = sent_ways(slot)
        for way in ways:
            @pl.when(conds[way])
            def _(way=way):
                tab_copy(src, slot, c, way).start()

    def start_own(c):
        src = lattice if c == lat_item else table.at[:, pl.ds(c * mc, mc)]
        pass_on(src, me, c)

    lat_own = pltpu.make_async_copy(lattice, lats.at[me], own_sem.at[chunks])
    lat_own.start()
    for c in (lat_item, 0, 1):
        start_own(c)
    own = [
        pltpu.make_async_copy(
            table.at[:, pl.ds(c * mc, mc)], gath.at[c, me], own_sem.at[c]
        )
        for c in range(chunks)
    ]
    for c in range(chunks):
        own[c].start()

    def tab_copy_all(ref, recv=None, send=None):
        return pltpu.make_async_remote_copy(
            src_ref=ref, dst_ref=ref,
            send_sem=send_sem.at[0, 0] if send is None else send,
            recv_sem=lat_recv.at[0, 0] if recv is None else recv,
            device_id={"band": other}, device_id_type=pl.DeviceIdType.MESH,
        )

    def along_mom(dist, c):
        for sign in (-1, 1):
            j = z + sign * dist

            @pl.when((j >= 0) & (j < moms))
            def _(j=j):
                slot = j * lat_n + x
                tab_copy(place(slot, c), slot, c, 0).wait_recv()
                pass_on(place(slot, c), slot, c)

    def from_lat(c):
        if lat_n == 2:
            every = lats if c == lat_item else gath.at[c]
            tab_copy_all(every.at[pl.ds(0, moms)], lat_recv.at[0, c]).wait_recv()
            return
        for dist in range(1, lat_n):
            for sign in (-1, 1):
                i = x + sign * dist

                @pl.when((i >= 0) & (i < lat_n))
                def _(i=i):
                    def one(j):
                        slot = j * lat_n + i
                        tab_copy(place(slot, c), slot, c, 2).wait_recv()
                        pass_on(place(slot, c), slot, c, (2, 3))

                    loop(moms, one)

    half = nb_loc
    rcopy.wait()
    rswap = pltpu.make_async_remote_copy(
        src_ref=rbuf.at[:, :, pl.ds(pl.multiple_of(other * half, 8), half)],
        dst_ref=rother, send_sem=swap_send.at[0], recv_sem=swap_recv.at[0],
        device_id={"band": other}, device_id_type=pl.DeviceIdType.MESH,
    )
    rswap.start()

    kq = pairs[:, pl.ds(pl.multiple_of(x * owned, 128), owned)]
    kq = kq.astype(F32).astype(BF16)

    def phase(q, carry):
        comp = lats[q].astype(F32).astype(BF16)
        turn = lax.dot_general(
            comp, kq, (((0,), (0,)), ((), ())), preferred_element_type=F32
        )
        turn = turn - jnp.round(turn * (1.0 / NK)) * NK
        cosine = quarter_sine(6.0 - jnp.abs(turn))
        folded = jnp.maximum(jnp.minimum(turn, 12.0 - turn), -12.0 - turn)
        sine = quarter_sine(folded)
        cb = cosine.astype(BF16)
        rows = pl.ds(pl.multiple_of(q * rloc, rloc), rloc)
        phase_a[rows, :owned] = cb
        phase_a[rows, owned:] = sine.astype(BF16)
        phase_b[rows, :owned] = (-sine).astype(BF16)
        phase_b[rows, owned:] = cb
        return carry


    group = math.gcd(shards, 8)
    kdim = group * rloc
    eights = nb_loc // 8

    def contract(c, g):
        pieces = [
            [gath[c, g * group + s, part].reshape(mc * nb_loc, rloc)
             for s in range(group)]
            for part in (0, 1)
        ]
        rows = pl.ds(g * kdim, kdim)
        return jnp.dot(
            jnp.concatenate(pieces[0], 1), phase_a[rows, :],
            preferred_element_type=F32,
        ) + jnp.dot(
            jnp.concatenate(pieces[1], 1), phase_b[rows, :],
            preferred_element_type=F32,
        )

    def band_swap(c):
        return pltpu.make_async_remote_copy(
            src_ref=bloch.at[c], dst_ref=bother.at[c],
            send_sem=swap_send.at[c + 1], recv_sem=swap_recv.at[c + 1],
            device_id={"band": other}, device_id_type=pl.DeviceIdType.MESH,
        )

    def right_part(bref, rref, row0, first):
        def body(lt, carry):
            l0 = pl.multiple_of(lt * 128, 128)
            lanes = pl.ds(l0, 128)
            lanes_im = pl.ds(l0 + owned, 128)
            for m0 in range(0, mc, mblk):
                cre = [None] * mblk
                cim = [None] * mblk
                for n in range(nb_loc):
                    vre = rref[0, n, pl.ds(row0, half), lanes]
                    vim = rref[1, n, pl.ds(row0, half), lanes]
                    for m in range(mblk):
                        at = (m0 + m) * eights + n // 8
                        row = pl.ds(n % 8, 1)
                        br = jnp.broadcast_to(bref[at, row, lanes], (half, 128))
                        bi = jnp.broadcast_to(bref[at, row, lanes_im], (half, 128))
                        a = br * vre - bi * vim
                        b = br * vim + bi * vre
                        cre[m] = a if n == 0 else cre[m] + a
                        cim[m] = b if n == 0 else cim[m] + b
                for m in range(mblk):
                    if not first:
                        cre[m] = cre[m] + mids[0, m0 + m, :, lanes]
                        cim[m] = cim[m] + mids[1, m0 + m, :, lanes]
                    mids[0, m0 + m, :, lanes] = cre[m]
                    mids[1, m0 + m, :, lanes] = cim[m]
            return carry

        lax.fori_loop(0, lane_tiles, body, 0)

    def left_part(c):
        def body(it, carry):
            eight = it // lane_tiles
            lanes = pl.ds(pl.multiple_of((it % lane_tiles) * 128, 128), 128)
            cre = [None] * 8
            cim = [None] * 8
            for m in range(mc):
                mre = mids[0, m, :, lanes]
                mim = mids[1, m, :, lanes]
                for k in range(8):
                    row = pl.ds(k, 1)
                    lr = jnp.broadcast_to(lbuf[0, c * mc + m, eight, row, lanes], (half, 128))
                    li = jnp.broadcast_to(lbuf[1, c * mc + m, eight, row, lanes], (half, 128))
                    a = lr * mre + li * mim
                    b = lr * mim - li * mre
                    cre[k] = a if m == 0 else cre[k] + a
                    cim[k] = b if m == 0 else cim[k] + b
            for k in range(8):
                at = eight * 8 + k
                if c > 0:
                    cre[k] = cre[k] + out[0, at, :, lanes]
                    cim[k] = cim[k] + out[1, at, :, lanes]
                out[0, at, :, lanes] = cre[k]
                out[1, at, :, lanes] = cim[k]
            return carry

        lax.fori_loop(0, (bands // 8) * lane_tiles, body, 0)

    mblk = min(mc, 8)

    def chunk(c):
        own[c].wait()
        from_lat(c)
        bloch[c] = contract(c, 0).reshape(bloch.shape[1:])
        if shards > group:
            def add(g, carry):
                bloch[c] += contract(c, g).reshape(bloch.shape[1:])
                return carry
            lax.fori_loop(1, shards // group, add, 0)
        band_swap(c).start()
        right_part(bloch.at[c], rbuf, pl.multiple_of(core * half, 8), True)
        if c == 0:
            rswap.wait_recv()
            lcopy.wait()
        band_swap(c).wait_recv()
        right_part(bother.at[c], rother, 0, False)
        left_part(c)

    for wave in range(1, chunks + moms + LAG):
        if wave < moms:
            along_mom(wave, lat_item)
        if 2 <= wave + 1 < chunks:
            start_own(wave + 1)
        for dist in range(1, moms):
            c = wave - dist
            if 0 <= c < chunks:
                along_mom(dist, c)
        if wave == moms:
            from_lat(lat_item)
            lat_own.wait()
            lax.fori_loop(0, shards, phase, 0)
        done = wave - moms - LAG
        if 0 <= done < chunks:
            chunk(done)

    for c in range(chunks):
        band_swap(c).wait_send()
    rswap.wait_send()

    def way_done(way, count, cond):
        @pl.when(cond)
        def _():
            tab_copy_all(
                gath.at[:, pl.ds(0, count)], send=send_sem.at[way, 0]
            ).wait_send()
            tab_copy_all(
                lats.at[pl.ds(0, count)], send=send_sem.at[way, 1]
            ).wait_send()

    for at in range(moms - 1):
        way_done(0, at + 1, z == at)
        way_done(1, at + 1, z == moms - 1 - at)
    for at in range(lat_n - 1):
        way_done(2, (at + 1) * moms, x == at)
        way_done(3, (at + 1) * moms, x == lat_n - 1 - at)


def per_device(moms, lat_n, table, lattice, pairs, left_rot, right_rotation):
    tab = jnp.transpose(table, (1, 2, 3, 0))
    lat = jnp.transpose(lattice, (1, 0))
    lef = jnp.transpose(left_rot, (1, 2, 3, 0))
    rig = jnp.transpose(right_rotation, (1, 2, 3, 0))
    bands = tab.shape[1]
    lef = lef.reshape(2, bands, bands // 8, 8, lef.shape[3])
    nb_loc = tab.shape[2]
    rloc = tab.shape[3]
    owned = rig.shape[3]
    shards = moms * lat_n
    chunks = 4
    mc = bands // chunks
    cfg = (moms, lat_n, chunks, mc, nb_loc, owned, bands)
    anyspace = pl.BlockSpec(memory_space=pl.ANY)
    vmem = pl.BlockSpec(memory_space=pltpu.VMEM)
    dma = pltpu.SemaphoreType.DMA
    res = pl.pallas_call(
        functools.partial(kernel, cfg),
        out_shape=pltpu.VMEM((2, bands, nb_loc, owned), F32),
        in_specs=[anyspace, anyspace, vmem, anyspace, anyspace],
        out_specs=vmem,
        scratch_shapes=[
            pltpu.VMEM((chunks, shards, 2, mc, nb_loc, rloc), BF16),
            pltpu.VMEM((shards, lat.shape[0], rloc), jnp.int32),
            pltpu.VMEM((shards * rloc, 2 * owned), BF16),
            pltpu.VMEM((shards * rloc, 2 * owned), BF16),
            pltpu.VMEM((chunks, mc * nb_loc // 8, 8, 2 * owned), F32),
            pltpu.VMEM((chunks, mc * nb_loc // 8, 8, 2 * owned), F32),
            pltpu.VMEM((2, mc, nb_loc, owned), F32),
            pltpu.VMEM(lef.shape, F32),
            pltpu.VMEM(rig.shape, F32),
            pltpu.VMEM((2, nb_loc, nb_loc, owned), F32),
            dma((4, 2)),
            dma((moms, chunks + 1)),
            dma((shards if lat_n > 2 else 1, chunks + 1)),
            dma((chunks + 1,)),
            dma((2,)),
            dma((chunks + 1,)),
            dma((chunks + 1,)),
        ],
        compiler_params=pltpu.CompilerParams(
            collective_id=0, has_side_effects=True,
            vmem_limit_bytes=60 * 1024 * 1024,
        ),
    )(tab, lat, pairs, lef, rig)
    return jnp.transpose(res, (3, 0, 1, 2))


def solution(mesh):
    in_specs = (
        P(("groups", "mom", "lat"), None, None, "band"),
        P(("mom", "lat"), None),
        P(None, ("groups", "mom")),
        P(("groups", "mom", "lat"), None, None, None),
        P(("groups", "mom", "lat"), None, "band", None),
    )
    out_specs = P(("groups", "mom", "lat"), None, None, "band")
    body = functools.partial(per_device, mesh.shape["mom"], mesh.shape["lat"])
    return jax.shard_map(
        body, mesh=mesh, in_specs=in_specs, out_specs=out_specs, check_vma=False
    )
```

time: 46.9 us -> 40.5 us (0.86)
  Pallas kernels: 44.4 us -> 39.3 us
  local copies, waits for them, and re-layouts: 2.26 us -> 0.97 us
    pallas_call x1, Pallas kernels: 44.4 us -> 39.3 us  [per_device(): pl.pallas_call(functools.partial(kernel, cfg), out_shape=pltpu.VMEM((2, b...]
    unnamed x1, local copies, waits for them, and re-layouts: 2.26 us -> 0.97 us
where the time goes in v1:
time: 40.5 us; the launch traced here: 40.2 us
  Pallas kernels  39.3 us (97%)
  local copies, waits for them, and re-layouts  0.97 us (2%)
    pallas_call x1, Pallas kernels, per_device(): pl.pallas_call(functools.partial(kernel, cfg), out_shape=pltpu.VMEM((2, b...  39.3 us
    unnamed x1, local copies, waits for them, and re-layouts  0.97 us

profile of v1, /device:TPU:0, one launch (start us, length us, event | category | flops | bytes accessed | tf_op | source)
XLA Modules:
  0.0 40.2 jit_solution(17910772515979531381)
XLA Ops:
  0.0 39.3 %shard_map.55 = f32[2,32,16,256]{3,2,1,0:T(8,128)S(1)} custom-call(bf16[2,32,16,128]{3,2,1,0:T(8,128)(2,1)} %bitcast.10, s32[6,128]{1,0:T(8,128)} %bitcast.11, s32[6,512]{1,0:T(8,128)} %pairs.1, f32[2,32,4,8,256]{4,3,2,1,0:T(8,128)} %bitcast.8, f32[2,16,32,256]{3,2,1,0:T(8,128)} %bitcast.9), custom_call_target="tpu_custom_call" | custom-call | tf_op jit(solution)/shard_map/pallas_call | solution.py:366
  39.3 1.0 %copy.7 = f32[256,2,32,16]{0,3,2,1:T(8,128)} copy(f32[256,2,32,16]{0,3,2,1:T(8,128)S(1)} %bitcast.7) | data formatting | bytes 2097152

commit v2 on v1

--- a/solution.py
+++ b/solution.py
@@ -229,7 +229,7 @@
             device_id={"band": other}, device_id_type=pl.DeviceIdType.MESH,
         )
 
-    def right_part(bref, rref, row0, first):
+    def right_part(bref, rref, row0, first, buf):
         def body(lt, carry):
             l0 = pl.multiple_of(lt * 128, 128)
             lanes = pl.ds(l0, 128)
@@ -251,23 +251,25 @@
                         cim[m] = b if n == 0 else cim[m] + b
                 for m in range(mblk):
                     if not first:
-                        cre[m] = cre[m] + mids[0, m0 + m, :, lanes]
-                        cim[m] = cim[m] + mids[1, m0 + m, :, lanes]
-                    mids[0, m0 + m, :, lanes] = cre[m]
-                    mids[1, m0 + m, :, lanes] = cim[m]
+                        cre[m] = cre[m] + mids[buf, 0, m0 + m, :, lanes]
+                        cim[m] = cim[m] + mids[buf, 1, m0 + m, :, lanes]
+                    mids[buf, 0, m0 + m, :, lanes] = cre[m]
+                    mids[buf, 1, m0 + m, :, lanes] = cim[m]
             return carry
 
         lax.fori_loop(0, lane_tiles, body, 0)
 
     def left_part(c):
+        buf = c % 2
+
         def body(it, carry):
             eight = it // lane_tiles
             lanes = pl.ds(pl.multiple_of((it % lane_tiles) * 128, 128), 128)
             cre = [None] * 8
             cim = [None] * 8
             for m in range(mc):
-                mre = mids[0, m, :, lanes]
-                mim = mids[1, m, :, lanes]
+                mre = mids[buf, 0, m, :, lanes]
+                mim = mids[buf, 1, m, :, lanes]
                 for k in range(8):
                     row = pl.ds(k, 1)
                     lr = jnp.broadcast_to(lbuf[0, c * mc + m, eight, row, lanes], (half, 128))
@@ -299,12 +301,18 @@
                 return carry
             lax.fori_loop(1, shards // group, add, 0)
         band_swap(c).start()
-        right_part(bloch.at[c], rbuf, pl.multiple_of(core * half, 8), True)
+        right_part(
+            bloch.at[c], rbuf, pl.multiple_of(core * half, 8), True, c % 2
+        )
+        if c > 0:
+            finish(c - 1)
+
+    def finish(c):
         if c == 0:
             rswap.wait_recv()
             lcopy.wait()
         band_swap(c).wait_recv()
-        right_part(bother.at[c], rother, 0, False)
+        right_part(bother.at[c], rother, 0, False, c % 2)
         left_part(c)
 
     for wave in range(1, chunks + moms + LAG):
@@ -323,6 +331,7 @@
         done = wave - moms - LAG
         if 0 <= done < chunks:
             chunk(done)
+    finish(chunks - 1)
 
     for c in range(chunks):
         band_swap(c).wait_send()
@@ -375,7 +384,7 @@
             pltpu.VMEM((shards * rloc, 2 * owned), BF16),
             pltpu.VMEM((chunks, mc * nb_loc // 8, 8, 2 * owned), F32),
             pltpu.VMEM((chunks, mc * nb_loc // 8, 8, 2 * owned), F32),
-            pltpu.VMEM((2, mc, nb_loc, owned), F32),
+            pltpu.VMEM((2, 2, mc, nb_loc, owned), F32),
             pltpu.VMEM(lef.shape, F32),
             pltpu.VMEM(rig.shape, F32),
             pltpu.VMEM((2, nb_loc, nb_loc, owned), F32),

time: 40.5 us -> 40.1 us (level)
  Pallas kernels: 39.3 us -> 38.8 us
    pallas_call x1, Pallas kernels: 39.3 us -> 38.8 us  [per_device(): pl.pallas_call(functools.partial(kernel, cfg), out_shape=pltpu.VMEM((2, b...]
where the time goes in v2:
time: 40.1 us; the launch traced here: 39.8 us
  Pallas kernels  38.8 us (97%)
  local copies, waits for them, and re-layouts  0.97 us (2%)
    pallas_call x1, Pallas kernels, per_device(): pl.pallas_call(functools.partial(kernel, cfg), out_shape=pltpu.VMEM((2, b...  38.8 us
    unnamed x1, local copies, waits for them, and re-layouts  0.97 us

profile of v2, /device:TPU:0, one launch (start us, length us, event | category | flops | bytes accessed | tf_op | source)
XLA Modules:
  0.0 39.8 jit_solution(32159136555019983)
XLA Ops:
  0.0 38.8 %shard_map.55 = f32[2,32,16,256]{3,2,1,0:T(8,128)S(1)} custom-call(bf16[2,32,16,128]{3,2,1,0:T(8,128)(2,1)} %bitcast.10, s32[6,128]{1,0:T(8,128)} %bitcast.11, s32[6,512]{1,0:T(8,128)} %pairs.1, f32[2,32,4,8,256]{4,3,2,1,0:T(8,128)} %bitcast.8, f32[2,16,32,256]{3,2,1,0:T(8,128)} %bitcast.9), custom_call_target="tpu_custom_call" | custom-call | tf_op jit(solution)/shard_map/pallas_call | solution.py:375
  38.8 1.0 %copy.7 = f32[256,2,32,16]{0,3,2,1:T(8,128)} copy(f32[256,2,32,16]{0,3,2,1:T(8,128)S(1)} %bitcast.7) | data formatting | bytes 2097152
